TPU v7x, 128 devices: a whole 4x4x4 slice. The times are simulated.
128 devices in a mesh: rows: 64 (over y, z, x), cols: 2 (over core).
Axes of the slice: x: 4, y: 4, z: 4, core: 2. Of those that a mesh axis runs over, the one named last changes fastest.
Arguments:
- video: bfloat16 [512, 256, 256], P('rows', 'cols'), may hold values from -12 to 12
- foreground: float32 [512, 256, 256], P('rows', 'cols'), may hold values from -4 to 4
- scaled_dual: float32 [512, 256, 256], P('rows', 'cols'), may hold values from -2.5 to 2.5
Outputs:
- background: float32 [512, 256, 256], P('rows', 'cols')
- new_foreground: float32 [512, 256, 256], P('rows', 'cols')
- new_dual: float32 [512, 256, 256], P('rows', 'cols')
All inputs are finite; a program needn't handle non-finite values.
Results may differ from a plain program's by a relative error of at most 0.00035.
Values sent between devices are 32-bit elements; how exact they have to be, the bound alone decides.
A program may use at most 64 MiB of HBM per device.

v0:
```python
import jax
import jax.numpy as jnp
from jax import lax
from jax.sharding import PartitionSpec as P

K_ROOT = 8
K_SIGN = 6
K_TV = 8
threshold_ratio = 1.0
dual_step = 0.25
tv_weight = 1.0


def shifted(x, axis, by):
    length = lax.axis_size(axis)
    pairs = [(i, i + by) for i in range(length) if 0 <= i + by < length]
    return lax.ppermute(x, axis, pairs)


def matmul(left, right):
    return jnp.dot(left, right, precision=lax.Precision.HIGHEST, preferred_element_type=jnp.float32)


def shrink_matrix(gram):
    size = gram.shape[0]
    identity = jnp.eye(size, dtype=jnp.float32)
    scale = jnp.sqrt(jnp.sum(gram * gram))
    root = gram / scale
    inverse = identity
    for sweep in range(K_ROOT):
        factor = 1.5 * identity - 0.5 * matmul(inverse, root)
        root = matmul(root, factor)
        inverse = matmul(factor, inverse)
    cutoff = threshold_ratio * jnp.trace(root) / size
    signed = root - cutoff * identity
    for sweep in range(K_SIGN):
        signed = 1.5 * signed - 0.5 * matmul(signed, matmul(signed, signed))
    return 0.5 * matmul(identity - cutoff * inverse, identity + signed)


def per_device(video, foreground, scaled_dual):
    rows_here, cols_here, frames = foreground.shape
    observed = video.astype(jnp.float32)
    mixed = observed - foreground + scaled_dual
    flat = mixed.reshape(-1, frames)
    gram = lax.psum(matmul(flat.T, flat), ("rows", "cols"))
    shrink = shrink_matrix(gram)
    background = matmul(flat, shrink).reshape(foreground.shape)
    target = observed - background + scaled_dual
    last_row = lax.axis_index("rows") == lax.axis_size("rows") - 1
    last_col = lax.axis_index("cols") == lax.axis_size("cols") - 1
    row_iota = lax.broadcasted_iota(jnp.int32, (rows_here, 1, 1), 0)
    col_iota = lax.broadcasted_iota(jnp.int32, (1, cols_here, 1), 1)
    row_keep = jnp.where(last_row & (row_iota == rows_here - 1), 0.0, 1.0).astype(jnp.float32)
    col_keep = jnp.where(last_col & (col_iota == cols_here - 1), 0.0, 1.0).astype(jnp.float32)
    dual_x = jnp.zeros_like(target)
    dual_y = jnp.zeros_like(target)

    def current_of(px, py):
        prev_x = shifted(px[-1:], "rows", 1)
        prev_y = shifted(py[:, -1:], "cols", 1)
        before_x = jnp.concatenate([prev_x, px[:-1]], axis=0)
        before_y = jnp.concatenate([prev_y, py[:, :-1]], axis=1)
        return target - (before_x - px + before_y - py)

    for sweep in range(K_TV):
        current = current_of(dual_x, dual_y)
        below = shifted(current[:1], "rows", -1)
        beside = shifted(current[:, :1], "cols", -1)
        down = (jnp.concatenate([current[1:], below], axis=0) - current) * row_keep
        across = (jnp.concatenate([current[:, 1:], beside], axis=1) - current) * col_keep
        dual_x = jnp.clip(dual_x + dual_step * down, -tv_weight, tv_weight)
        dual_y = jnp.clip(dual_y + dual_step * across, -tv_weight, tv_weight)
    new_foreground = current_of(dual_x, dual_y)
    new_dual = scaled_dual + observed - background - new_foreground
    return (background, new_foreground, new_dual)


def solution(mesh):
    return jax.shard_map(
        per_device,
        mesh=mesh,
        in_specs=(P("rows", "cols", None), P("rows", "cols", None), P("rows", "cols", None)),
        out_specs=(P("rows", "cols", None), P("rows", "cols", None), P("rows", "cols", None)),
        check_vma=False,
    )
```

profile of v0, /device:TPU:8, one launch (start us, length us, event | category | flops | bytes accessed | tf_op | source)
XLA Modules:
  0.0 340.7 jit_solution(16229040897291042421)
XLA Ops:
  7.2 5.1 %convolution_bitcast_fusion = f32[256,256]{1,0:T(8,128)} fusion(f32[8,128,256]{2,1,0:T(8,128)} %param.5, f32[8,128,256]{2,1,0:T(8,128)} %param.4, bf16[8,128,256]{2,1,0:T(8,128)(2,1)} %param.3), kind=kOutput, calls=%fused_computation.36 | convolution fusion | flops 806092800 | bytes 2883584 | tf_op jit(solution)/shard_map/dot_general | solution.py:21
  14.1 3.4 collective-permute-start
  17.5 140.5 %all-reduce.4.cloned.1.call-done = f32[256,256]{1,0:T(8,128)} async-done(((f32[256,256]{1,0:T(8,128)}), f32[256,256]{1,0:T(8,128)}) %all-reduce.4.cloned.1.call-update) | async-done | bytes 262160 | tf_op jit(solution)/shard_map/psum | solution.py:46
  176.9 2.0 add_subtract_fusion
  178.9 5.3 %collective-permute-start.2 = (f32[1,128,256]{2,1,0:T(8,128)S(1)}, f32[1,128,256]{2,1,0:T(8,128)S(1)}, u32[]{:S(2)}, u32[]{:S(2)}) collective-permute-start(f32[1,128,256]{2,1,0:T(8,128)S(1)} %slice.267), channel_id=1, source_target_pairs={{2,0},{4,2},{6,4},{8,6},{10,8},{12,10},{14,12},{16,14},{18,16},{20... | collective-permute-start | bytes 393224 | tf_op jit(solution)/shard_map/ppermute | solution.py:17
  187.7 2.1 collective-permute-start.3
  189.9 1.9 collective-permute-start.5
  192.6 6.8 %collective-permute-done.3 = f32[1,128,256]{2,1,0:T(8,128)S(1)} collective-permute-done((f32[1,128,256]{2,1,0:T(8,128)S(1)}, f32[1,128,256]{2,1,0:T(8,128)S(1)}, u32[]{:S(2)}, u32[]{:S(2)}) %collective-permute-start.3) | collective-permute-done | bytes 131104 | tf_op jit(solution)/shard_map/ppermute | solution.py:17
  199.8 3.5 %collective-permute-start.6 = (f32[1,128,256]{2,1,0:T(8,128)S(1)}, f32[1,128,256]{2,1,0:T(8,128)S(1)}, u32[]{:S(2)}, u32[]{:S(2)}) collective-permute-start(f32[1,128,256]{2,1,0:T(8,128)S(1)} %slice.275), channel_id=1, source_target_pairs={{2,0},{4,2},{6,4},{8,6},{10,8},{12,10},{14,12},{16,14},{18,16},{20... | collective-permute-start | bytes 393224 | tf_op jit(solution)/shard_map/ppermute | solution.py:17
  207.2 2.1 collective-permute-start.7
  209.3 1.8 collective-permute-start.9
  211.9 6.7 %collective-permute-done.7 = f32[1,128,256]{2,1,0:T(8,128)S(1)} collective-permute-done((f32[1,128,256]{2,1,0:T(8,128)S(1)}, f32[1,128,256]{2,1,0:T(8,128)S(1)}, u32[]{:S(2)}, u32[]{:S(2)}) %collective-permute-start.7) | collective-permute-done | bytes 131104 | tf_op jit(solution)/shard_map/ppermute | solution.py:17
  219.0 3.2 collective-permute-start.10
  226.4 2.1 collective-permute-start.11
  231.1 6.4 %collective-permute-done.11 = f32[1,128,256]{2,1,0:T(8,128)S(1)} collective-permute-done((f32[1,128,256]{2,1,0:T(8,128)S(1)}, f32[1,128,256]{2,1,0:T(8,128)S(1)}, u32[]{:S(2)}, u32[]{:S(2)}) %collective-permute-start.11) | collective-permute-done | bytes 131104 | tf_op jit(solution)/shard_map/ppermute | solution.py:17
  237.9 3.2 collective-permute-start.14
  245.3 2.1 collective-permute-start.15
  250.0 6.4 %collective-permute-done.15 = f32[1,128,256]{2,1,0:T(8,128)S(1)} collective-permute-done((f32[1,128,256]{2,1,0:T(8,128)S(1)}, f32[1,128,256]{2,1,0:T(8,128)S(1)}, u32[]{:S(2)}, u32[]{:S(2)}) %collective-permute-start.15) | collective-permute-done | bytes 131104 | tf_op jit(solution)/shard_map/ppermute | solution.py:17
  256.7 3.2 collective-permute-start.18
  264.1 2.1 collective-permute-start.19
  268.8 6.4 %collective-permute-done.19 = f32[1,128,256]{2,1,0:T(8,128)S(1)} collective-permute-done((f32[1,128,256]{2,1,0:T(8,128)S(1)}, f32[1,128,256]{2,1,0:T(8,128)S(1)}, u32[]{:S(2)}, u32[]{:S(2)}) %collective-permute-start.19) | collective-permute-done | bytes 131104 | tf_op jit(solution)/shard_map/ppermute | solution.py:17
  275.6 3.2 collective-permute-start.22
  283.0 2.1 collective-permute-start.23
  287.7 6.4 %collective-permute-done.23 = f32[1,128,256]{2,1,0:T(8,128)S(1)} collective-permute-done((f32[1,128,256]{2,1,0:T(8,128)S(1)}, f32[1,128,256]{2,1,0:T(8,128)S(1)}, u32[]{:S(2)}, u32[]{:S(2)}) %collective-permute-start.23) | collective-permute-done | bytes 131104 | tf_op jit(solution)/shard_map/ppermute | solution.py:17
  294.4 3.2 collective-permute-start.26
  301.8 2.1 collective-permute-start.27
  306.5 6.4 %collective-permute-done.27 = f32[1,128,256]{2,1,0:T(8,128)S(1)} collective-permute-done((f32[1,128,256]{2,1,0:T(8,128)S(1)}, f32[1,128,256]{2,1,0:T(8,128)S(1)}, u32[]{:S(2)}, u32[]{:S(2)}) %collective-permute-start.27) | collective-permute-done | bytes 131104 | tf_op jit(solution)/shard_map/ppermute | solution.py:17
  313.3 3.2 collective-permute-start.30
  320.7 2.2 collective-permute-start.31
  323.0 1.9 collective-permute-start.33
  325.7 6.2 %collective-permute-done.31 = f32[1,128,256]{2,1,0:T(8,128)S(1)} collective-permute-done((f32[1,128,256]{2,1,0:T(8,128)S(1)}, f32[1,128,256]{2,1,0:T(8,128)S(1)}, u32[]{:S(2)}, u32[]{:S(2)}) %collective-permute-start.31) | collective-permute-done | bytes 131104 | tf_op jit(solution)/shard_map/ppermute | solution.py:17
  332.0 1.9 fusion.20
  (167 shorter events, 69.3 us)
Async XLA Ops:
  7.2 150.9 %all-reduce.4.cloned.1.call-start = ((), (), s32[]{:S(2)}) async-start(), calls=%async_computation | async-start | bytes 524288 | tf_op jit(solution)/shard_map/psum | solution.py:46
  12.4 163.8 %collective-permute-start.1 = (f32[8,1,256]{2,1,0:T(1,128)S(1)}, f32[8,1,256]{2,1,0:T(1,128)S(1)}, u32[]{:S(2)}, u32[]{:S(2)}) collective-permute-start(f32[8,1,256]{2,1,0:T(1,128)S(1)} %slice.201), channel_id=1, source_target_pairs={{0,1},{2,3},{4,5},{6,7},{8,9},{10,11},{12,13},{14,15},{16,17},{18,... | collective-permute-start | bytes 24584 | tf_op jit(solution)/shard_map/ppermute | solution.py:17
  14.1 162.0 %collective-permute-start = (f32[1,128,256]{2,1,0:T(8,128)S(1)}, f32[1,128,256]{2,1,0:T(8,128)S(1)}, u32[]{:S(2)}, u32[]{:S(2)}) collective-permute-start(f32[1,128,256]{2,1,0:T(8,128)S(1)} %slice.200), channel_id=1, source_target_pairs={{0,2},{2,4},{4,6},{6,8},{8,10},{10,12},{12,14},{14,16},{16,18},{18... | collective-permute-start | bytes 393224 | tf_op jit(solution)/shard_map/ppermute | solution.py:17
  178.9 8.4 %collective-permute-start.2 = (f32[1,128,256]{2,1,0:T(8,128)S(1)}, f32[1,128,256]{2,1,0:T(8,128)S(1)}, u32[]{:S(2)}, u32[]{:S(2)}) collective-permute-start(f32[1,128,256]{2,1,0:T(8,128)S(1)} %slice.267), channel_id=1, source_target_pairs={{2,0},{4,2},{6,4},{8,6},{10,8},{12,10},{14,12},{16,14},{18,16},{20... | collective-permute-start | bytes 393224 | tf_op jit(solution)/shard_map/ppermute | solution.py:17
  184.2 3.1 collective-permute-start.4
  187.7 11.7 %collective-permute-start.3 = (f32[1,128,256]{2,1,0:T(8,128)S(1)}, f32[1,128,256]{2,1,0:T(8,128)S(1)}, u32[]{:S(2)}, u32[]{:S(2)}) collective-permute-start(f32[1,128,256]{2,1,0:T(8,128)S(1)} %slice.268), channel_id=1, source_target_pairs={{0,2},{2,4},{4,6},{6,8},{8,10},{10,12},{12,14},{14,16},{16,18},{18... | collective-permute-start | bytes 393224 | tf_op jit(solution)/shard_map/ppermute | solution.py:17
  189.9 2.7 collective-permute-start.5
  199.8 6.9 %collective-permute-start.6 = (f32[1,128,256]{2,1,0:T(8,128)S(1)}, f32[1,128,256]{2,1,0:T(8,128)S(1)}, u32[]{:S(2)}, u32[]{:S(2)}) collective-permute-start(f32[1,128,256]{2,1,0:T(8,128)S(1)} %slice.275), channel_id=1, source_target_pairs={{2,0},{4,2},{6,4},{8,6},{10,8},{12,10},{14,12},{16,14},{18,16},{20... | collective-permute-start | bytes 393224 | tf_op jit(solution)/shard_map/ppermute | solution.py:17
  203.4 3.1 collective-permute-start.8
  207.2 11.5 %collective-permute-start.7 = (f32[1,128,256]{2,1,0:T(8,128)S(1)}, f32[1,128,256]{2,1,0:T(8,128)S(1)}, u32[]{:S(2)}, u32[]{:S(2)}) collective-permute-start(f32[1,128,256]{2,1,0:T(8,128)S(1)} %slice.276), channel_id=1, source_target_pairs={{0,2},{2,4},{4,6},{6,8},{8,10},{10,12},{12,14},{14,16},{16,18},{18... | collective-permute-start | bytes 393224 | tf_op jit(solution)/shard_map/ppermute | solution.py:17
  209.3 2.6 collective-permute-start.9
  219.0 6.9 %collective-permute-start.10 = (f32[1,128,256]{2,1,0:T(8,128)S(1)}, f32[1,128,256]{2,1,0:T(8,128)S(1)}, u32[]{:S(2)}, u32[]{:S(2)}) collective-permute-start(f32[1,128,256]{2,1,0:T(8,128)S(1)} %slice.283), channel_id=1, source_target_pairs={{2,0},{4,2},{6,4},{8,6},{10,8},{12,10},{14,12},{16,14},{18,16},{20... | collective-permute-start | bytes 393224 | tf_op jit(solution)/shard_map/ppermute | solution.py:17
  222.2 3.1 collective-permute-start.12
  226.4 11.1 %collective-permute-start.11 = (f32[1,128,256]{2,1,0:T(8,128)S(1)}, f32[1,128,256]{2,1,0:T(8,128)S(1)}, u32[]{:S(2)}, u32[]{:S(2)}) collective-permute-start(f32[1,128,256]{2,1,0:T(8,128)S(1)} %slice.284), channel_id=1, source_target_pairs={{0,2},{2,4},{4,6},{6,8},{8,10},{10,12},{12,14},{14,16},{16,18},{18... | collective-permute-start | bytes 393224 | tf_op jit(solution)/shard_map/ppermute | solution.py:17
  228.5 2.6 collective-permute-start.13
  237.9 6.9 %collective-permute-start.14 = (f32[1,128,256]{2,1,0:T(8,128)S(1)}, f32[1,128,256]{2,1,0:T(8,128)S(1)}, u32[]{:S(2)}, u32[]{:S(2)}) collective-permute-start(f32[1,128,256]{2,1,0:T(8,128)S(1)} %slice.291), channel_id=1, source_target_pairs={{2,0},{4,2},{6,4},{8,6},{10,8},{12,10},{14,12},{16,14},{18,16},{20... | collective-permute-start | bytes 393224 | tf_op jit(solution)/shard_map/ppermute | solution.py:17
  241.1 3.1 collective-permute-start.16
  245.3 11.1 %collective-permute-start.15 = (f32[1,128,256]{2,1,0:T(8,128)S(1)}, f32[1,128,256]{2,1,0:T(8,128)S(1)}, u32[]{:S(2)}, u32[]{:S(2)}) collective-permute-start(f32[1,128,256]{2,1,0:T(8,128)S(1)} %slice.292), channel_id=1, source_target_pairs={{0,2},{2,4},{4,6},{6,8},{8,10},{10,12},{12,14},{14,16},{16,18},{18... | collective-permute-start | bytes 393224 | tf_op jit(solution)/shard_map/ppermute | solution.py:17
  247.4 2.6 collective-permute-start.17
  256.7 6.9 %collective-permute-start.18 = (f32[1,128,256]{2,1,0:T(8,128)S(1)}, f32[1,128,256]{2,1,0:T(8,128)S(1)}, u32[]{:S(2)}, u32[]{:S(2)}) collective-permute-start(f32[1,128,256]{2,1,0:T(8,128)S(1)} %slice.299), channel_id=1, source_target_pairs={{2,0},{4,2},{6,4},{8,6},{10,8},{12,10},{14,12},{16,14},{18,16},{20... | collective-permute-start | bytes 393224 | tf_op jit(solution)/shard_map/ppermute | solution.py:17
  259.9 3.1 collective-permute-start.20
  264.1 11.1 %collective-permute-start.19 = (f32[1,128,256]{2,1,0:T(8,128)S(1)}, f32[1,128,256]{2,1,0:T(8,128)S(1)}, u32[]{:S(2)}, u32[]{:S(2)}) collective-permute-start(f32[1,128,256]{2,1,0:T(8,128)S(1)} %slice.300), channel_id=1, source_target_pairs={{0,2},{2,4},{4,6},{6,8},{8,10},{10,12},{12,14},{14,16},{16,18},{18... | collective-permute-start | bytes 393224 | tf_op jit(solution)/shard_map/ppermute | solution.py:17
  275.6 6.9 %collective-permute-start.22 = (f32[1,128,256]{2,1,0:T(8,128)S(1)}, f32[1,128,256]{2,1,0:T(8,128)S(1)}, u32[]{:S(2)}, u32[]{:S(2)}) collective-permute-start(f32[1,128,256]{2,1,0:T(8,128)S(1)} %slice.307), channel_id=1, source_target_pairs={{2,0},{4,2},{6,4},{8,6},{10,8},{12,10},{14,12},{16,14},{18,16},{20... | collective-permute-start | bytes 393224 | tf_op jit(solution)/shard_map/ppermute | solution.py:17
  278.8 3.1 collective-permute-start.24
  283.0 11.1 %collective-permute-start.23 = (f32[1,128,256]{2,1,0:T(8,128)S(1)}, f32[1,128,256]{2,1,0:T(8,128)S(1)}, u32[]{:S(2)}, u32[]{:S(2)}) collective-permute-start(f32[1,128,256]{2,1,0:T(8,128)S(1)} %slice.308), channel_id=1, source_target_pairs={{0,2},{2,4},{4,6},{6,8},{8,10},{10,12},{12,14},{14,16},{16,18},{18... | collective-permute-start | bytes 393224 | tf_op jit(solution)/shard_map/ppermute | solution.py:17
  294.4 6.9 %collective-permute-start.26 = (f32[1,128,256]{2,1,0:T(8,128)S(1)}, f32[1,128,256]{2,1,0:T(8,128)S(1)}, u32[]{:S(2)}, u32[]{:S(2)}) collective-permute-start(f32[1,128,256]{2,1,0:T(8,128)S(1)} %slice.315), channel_id=1, source_target_pairs={{2,0},{4,2},{6,4},{8,6},{10,8},{12,10},{14,12},{16,14},{18,16},{20... | collective-permute-start | bytes 393224 | tf_op jit(solution)/shard_map/ppermute | solution.py:17
  297.6 3.1 collective-permute-start.28
  301.8 11.1 %collective-permute-start.27 = (f32[1,128,256]{2,1,0:T(8,128)S(1)}, f32[1,128,256]{2,1,0:T(8,128)S(1)}, u32[]{:S(2)}, u32[]{:S(2)}) collective-permute-start(f32[1,128,256]{2,1,0:T(8,128)S(1)} %slice.316), channel_id=1, source_target_pairs={{0,2},{2,4},{4,6},{6,8},{8,10},{10,12},{12,14},{14,16},{16,18},{18... | collective-permute-start | bytes 393224 | tf_op jit(solution)/shard_map/ppermute | solution.py:17
  313.3 6.9 %collective-permute-start.30 = (f32[1,128,256]{2,1,0:T(8,128)S(1)}, f32[1,128,256]{2,1,0:T(8,128)S(1)}, u32[]{:S(2)}, u32[]{:S(2)}) collective-permute-start(f32[1,128,256]{2,1,0:T(8,128)S(1)} %slice.323), channel_id=1, source_target_pairs={{2,0},{4,2},{6,4},{8,6},{10,8},{12,10},{14,12},{16,14},{18,16},{20... | collective-permute-start | bytes 393224 | tf_op jit(solution)/shard_map/ppermute | solution.py:17
  316.5 3.1 collective-permute-start.32
  320.7 11.2 %collective-permute-start.31 = (f32[1,128,256]{2,1,0:T(8,128)S(1)}, f32[1,128,256]{2,1,0:T(8,128)S(1)}, u32[]{:S(2)}, u32[]{:S(2)}) collective-permute-start(f32[1,128,256]{2,1,0:T(8,128)S(1)} %slice.324), channel_id=1, source_target_pairs={{0,2},{2,4},{4,6},{6,8},{8,10},{10,12},{12,14},{14,16},{16,18},{18... | collective-permute-start | bytes 393224 | tf_op jit(solution)/shard_map/ppermute | solution.py:17
  323.0 2.7 collective-permute-start.33
  (9 other events, 34.7 us)
Sparse Core Ops, SparseCore 0:
  13.3 144.7 all-reduce.3
where the time goes:
time: 342 us; the launch traced here: 341 us
  waiting for transfers between devices  214 us (63%)
  starting transfers between devices  74.6 us (22%)
  matrix products  21.9 us (6%)
  between operations  16.6 us (5%)
  other arithmetic  10.1 us (3%)
    psum x1, waiting for transfers between devices, per_device(): gram = lax.psum(matmul(flat.T, flat), ('rows', 'cols'))  141 us
    ppermute x34, starting transfers between devices, shifted(): return lax.ppermute(x, axis, pairs)  74.6 us
    ppermute x34, waiting for transfers between devices, shifted(): return lax.ppermute(x, axis, pairs)  74 us
    dot_general x39, matrix products, matmul(): jnp.dot(left, right, precision=lax.Precision.HIGHEST, preferred_element_t...  21.9 us
  transfers between devices with their start and end apart: 35, of which 32 were waited for; matrix products, arithmetic and copies ran while one was open for 5% of the time, Pallas kernels for 0%

commit v1 on v0

--- a/solution.py
+++ b/solution.py
@@ -43,7 +43,7 @@
     observed = video.astype(jnp.float32)
     mixed = observed - foreground + scaled_dual
     flat = mixed.reshape(-1, frames)
-    gram = lax.psum(matmul(flat.T, flat), ("rows", "cols"))
+    gram = jnp.sum(lax.all_gather(matmul(flat.T, flat), ("rows", "cols")), axis=0)
     shrink = shrink_matrix(gram)
     background = matmul(flat, shrink).reshape(foreground.shape)
     target = observed - background + scaled_dual

time: 342 us -> 317 us (0.927)
  waiting for transfers between devices: 214 us -> 178 us
  other arithmetic: 10.1 us -> 21.5 us
    psum x1 -> x0, waiting for transfers between devices: 141 us -> none  [per_device(): gram = lax.psum(matmul(flat.T, flat), ('rows', 'cols'))]
    all_gather x0 -> x1, waiting for transfers between devices: none -> 104 us  [per_device(): lax.all_gather(matmul(flat.T, flat), ('rows', 'cols'))]
    reduce_sum x0 -> x1, other arithmetic: none -> 12.1 us  [per_device(): jnp.sum(lax.all_gather(matmul(flat.T, flat), ('rows', 'cols')), axis=0)]
  transfers between devices with their start and end apart: 35 -> 35, of which waited for: 32 -> 32; matrix products, arithmetic and copies ran while one was open for 5% -> 9% of each run, Pallas kernels for 0% -> 0%
where the time goes in v1:
time: 317 us; the launch traced here: 316 us
  waiting for transfers between devices  178 us (56%)
  starting transfers between devices  74.4 us (23%)
  matrix products  23.5 us (7%)
  other arithmetic  21.5 us (7%)
  between operations  16.5 us (5%)
    all_gather x1, waiting for transfers between devices, per_device(): lax.all_gather(matmul(flat.T, flat), ('rows', 'cols'))  104 us
    ppermute x34, starting transfers between devices, shifted(): return lax.ppermute(x, axis, pairs)  74.4 us
    ppermute x34, waiting for transfers between devices, shifted(): return lax.ppermute(x, axis, pairs)  74.1 us
    dot_general x39, matrix products, matmul(): jnp.dot(left, right, precision=lax.Precision.HIGHEST, preferred_element_t...  23.5 us
    reduce_sum x1, other arithmetic, per_device(): jnp.sum(lax.all_gather(matmul(flat.T, flat), ('rows', 'cols')), axis=0)  12.1 us
  transfers between devices with their start and end apart: 35, of which 32 were waited for; matrix products, arithmetic and copies ran while one was open for 9% of the time, Pallas kernels for 0%

profile of v1, /device:TPU:8, one launch (start us, length us, event | category | flops | bytes accessed | tf_op | source)
XLA Modules:
  0.0 316.3 jit_solution(13586562370315680722)
XLA Ops:
  7.2 5.2 %convolution_bitcast_fusion = f32[256,256]{1,0:T(8,128)} fusion(f32[8,128,256]{2,1,0:T(8,128)} %param.5, f32[8,128,256]{2,1,0:T(8,128)} %param.4, bf16[8,128,256]{2,1,0:T(8,128)(2,1)} %param.3), kind=kOutput, calls=%fused_computation.36 | convolution fusion | flops 806092800 | bytes 2883584 | tf_op jit(solution)/shard_map/dot_general | solution.py:21
  12.5 3.4 %collective-permute-start = (f32[1,128,256]{2,1,0:T(8,128)S(1)}, f32[1,128,256]{2,1,0:T(8,128)S(1)}, u32[]{:S(2)}, u32[]{:S(2)}) collective-permute-start(f32[1,128,256]{2,1,0:T(8,128)S(1)} %slice.200), channel_id=1, source_target_pairs={{0,2},{2,4},{4,6},{6,8},{8,10},{10,12},{12,14},{14,16},{16,18},{18... | collective-permute-start | bytes 393224 | tf_op jit(solution)/shard_map/ppermute | solution.py:17
  17.4 103.8 %all-gather.3.cloned.1.call-done = f32[32768,256]{1,0:T(8,128)} async-done(((f32[256,256]{1,0:T(8,128)}), f32[32768,256]{1,0:T(8,128)}) %all-gather.3.cloned.1.call-update) | async-done | bytes 33554448 | tf_op jit(solution)/shard_map/all_gather | solution.py:46
  121.2 12.1 %reduce_sum.28 = f32[256,256]{1,0:T(8,128)S(1)} reduce(f32[128,256,256]{2,1,0:T(8,128)} %bitcast.81, f32[]{:T(128)} %constant.13.clone.1), dimensions={0}, to_apply=%region_0.0 | reduce | flops 8323072 | bytes 33816580 | tf_op jit(solution)/shard_map/reduce_sum | solution.py:46
  150.5 3.5 %add_subtract_fusion = (f32[8,128,256]{2,1,0:T(8,128)S(1)}, f32[8,128,256]{2,1,0:T(8,128)S(1)}, f32[8,128,256]{2,1,0:T(8,128)}) fusion(f32[8,1,256]{2,1,0:T(1,128)S(1)} %collective-permute-done.1, f32[1,128,256]{2,1,0:T(8,128)S(1)} %collective-permute-done, f32[8,128,256]{2,1,0:T(8,128)S(1)} %copy-done, bf16[8,128,256]{2,1,0:T(8,128)(2,1)} %param.3, ...), kind=kOutput, calls=%fused_computation.151 | convolution fusion | flops 807403520 | bytes 6168576 | tf_op jit(solution)/shard_map/dot_general | solution.py:21
  154.0 5.3 %collective-permute-start.2 = (f32[1,128,256]{2,1,0:T(8,128)S(1)}, f32[1,128,256]{2,1,0:T(8,128)S(1)}, u32[]{:S(2)}, u32[]{:S(2)}) collective-permute-start(f32[1,128,256]{2,1,0:T(8,128)S(1)} %slice.267), channel_id=1, source_target_pairs={{2,0},{4,2},{6,4},{8,6},{10,8},{12,10},{14,12},{16,14},{18,16},{20... | collective-permute-start | bytes 393224 | tf_op jit(solution)/shard_map/ppermute | solution.py:17
  163.0 2.5 collective-permute-start.3
  167.7 6.9 %collective-permute-done.3 = f32[1,128,256]{2,1,0:T(8,128)S(1)} collective-permute-done((f32[1,128,256]{2,1,0:T(8,128)S(1)}, f32[1,128,256]{2,1,0:T(8,128)S(1)}, u32[]{:S(2)}, u32[]{:S(2)}) %collective-permute-start.3) | collective-permute-done | bytes 131104 | tf_op jit(solution)/shard_map/ppermute | solution.py:17
  175.0 3.8 %collective-permute-start.6 = (f32[1,128,256]{2,1,0:T(8,128)S(1)}, f32[1,128,256]{2,1,0:T(8,128)S(1)}, u32[]{:S(2)}, u32[]{:S(2)}) collective-permute-start(f32[1,128,256]{2,1,0:T(8,128)S(1)} %slice.275), channel_id=1, source_target_pairs={{2,0},{4,2},{6,4},{8,6},{10,8},{12,10},{14,12},{16,14},{18,16},{20... | collective-permute-start | bytes 393224 | tf_op jit(solution)/shard_map/ppermute | solution.py:17
  182.4 2.0 collective-permute-start.7
  184.5 2.0 collective-permute-start.9
  187.3 6.8 %collective-permute-done.7 = f32[1,128,256]{2,1,0:T(8,128)S(1)} collective-permute-done((f32[1,128,256]{2,1,0:T(8,128)S(1)}, f32[1,128,256]{2,1,0:T(8,128)S(1)}, u32[]{:S(2)}, u32[]{:S(2)}) %collective-permute-start.7) | collective-permute-done | bytes 131104 | tf_op jit(solution)/shard_map/ppermute | solution.py:17
  194.5 3.2 %collective-permute-start.10 = (f32[1,128,256]{2,1,0:T(8,128)S(1)}, f32[1,128,256]{2,1,0:T(8,128)S(1)}, u32[]{:S(2)}, u32[]{:S(2)}) collective-permute-start(f32[1,128,256]{2,1,0:T(8,128)S(1)} %slice.283), channel_id=1, source_target_pairs={{2,0},{4,2},{6,4},{8,6},{10,8},{12,10},{14,12},{16,14},{18,16},{20... | collective-permute-start | bytes 393224 | tf_op jit(solution)/shard_map/ppermute | solution.py:17
  201.9 2.1 collective-permute-start.11
  204.0 1.8 collective-permute-start.13
  206.6 6.4 %collective-permute-done.11 = f32[1,128,256]{2,1,0:T(8,128)S(1)} collective-permute-done((f32[1,128,256]{2,1,0:T(8,128)S(1)}, f32[1,128,256]{2,1,0:T(8,128)S(1)}, u32[]{:S(2)}, u32[]{:S(2)}) %collective-permute-start.11) | collective-permute-done | bytes 131104 | tf_op jit(solution)/shard_map/ppermute | solution.py:17
  213.3 3.2 %collective-permute-start.14 = (f32[1,128,256]{2,1,0:T(8,128)S(1)}, f32[1,128,256]{2,1,0:T(8,128)S(1)}, u32[]{:S(2)}, u32[]{:S(2)}) collective-permute-start(f32[1,128,256]{2,1,0:T(8,128)S(1)} %slice.291), channel_id=1, source_target_pairs={{2,0},{4,2},{6,4},{8,6},{10,8},{12,10},{14,12},{16,14},{18,16},{20... | collective-permute-start | bytes 393224 | tf_op jit(solution)/shard_map/ppermute | solution.py:17
  220.7 2.1 collective-permute-start.15
  225.4 6.4 %collective-permute-done.15 = f32[1,128,256]{2,1,0:T(8,128)S(1)} collective-permute-done((f32[1,128,256]{2,1,0:T(8,128)S(1)}, f32[1,128,256]{2,1,0:T(8,128)S(1)}, u32[]{:S(2)}, u32[]{:S(2)}) %collective-permute-start.15) | collective-permute-done | bytes 131104 | tf_op jit(solution)/shard_map/ppermute | solution.py:17
  232.2 3.2 %collective-permute-start.18 = (f32[1,128,256]{2,1,0:T(8,128)S(1)}, f32[1,128,256]{2,1,0:T(8,128)S(1)}, u32[]{:S(2)}, u32[]{:S(2)}) collective-permute-start(f32[1,128,256]{2,1,0:T(8,128)S(1)} %slice.299), channel_id=1, source_target_pairs={{2,0},{4,2},{6,4},{8,6},{10,8},{12,10},{14,12},{16,14},{18,16},{20... | collective-permute-start | bytes 393224 | tf_op jit(solution)/shard_map/ppermute | solution.py:17
  239.7 2.1 collective-permute-start.19
  244.4 6.4 %collective-permute-done.19 = f32[1,128,256]{2,1,0:T(8,128)S(1)} collective-permute-done((f32[1,128,256]{2,1,0:T(8,128)S(1)}, f32[1,128,256]{2,1,0:T(8,128)S(1)}, u32[]{:S(2)}, u32[]{:S(2)}) %collective-permute-start.19) | collective-permute-done | bytes 131104 | tf_op jit(solution)/shard_map/ppermute | solution.py:17
  251.1 3.2 %collective-permute-start.22 = (f32[1,128,256]{2,1,0:T(8,128)S(1)}, f32[1,128,256]{2,1,0:T(8,128)S(1)}, u32[]{:S(2)}, u32[]{:S(2)}) collective-permute-start(f32[1,128,256]{2,1,0:T(8,128)S(1)} %slice.307), channel_id=1, source_target_pairs={{2,0},{4,2},{6,4},{8,6},{10,8},{12,10},{14,12},{16,14},{18,16},{20... | collective-permute-start | bytes 393224 | tf_op jit(solution)/shard_map/ppermute | solution.py:17
  258.6 2.1 collective-permute-start.23
  263.3 6.4 %collective-permute-done.23 = f32[1,128,256]{2,1,0:T(8,128)S(1)} collective-permute-done((f32[1,128,256]{2,1,0:T(8,128)S(1)}, f32[1,128,256]{2,1,0:T(8,128)S(1)}, u32[]{:S(2)}, u32[]{:S(2)}) %collective-permute-start.23) | collective-permute-done | bytes 131104 | tf_op jit(solution)/shard_map/ppermute | solution.py:17
  270.1 3.2 %collective-permute-start.26 = (f32[1,128,256]{2,1,0:T(8,128)S(1)}, f32[1,128,256]{2,1,0:T(8,128)S(1)}, u32[]{:S(2)}, u32[]{:S(2)}) collective-permute-start(f32[1,128,256]{2,1,0:T(8,128)S(1)} %slice.315), channel_id=1, source_target_pairs={{2,0},{4,2},{6,4},{8,6},{10,8},{12,10},{14,12},{16,14},{18,16},{20... | collective-permute-start | bytes 393224 | tf_op jit(solution)/shard_map/ppermute | solution.py:17
  277.5 2.1 collective-permute-start.27
  282.3 6.4 %collective-permute-done.27 = f32[1,128,256]{2,1,0:T(8,128)S(1)} collective-permute-done((f32[1,128,256]{2,1,0:T(8,128)S(1)}, f32[1,128,256]{2,1,0:T(8,128)S(1)}, u32[]{:S(2)}, u32[]{:S(2)}) %collective-permute-start.27) | collective-permute-done | bytes 131104 | tf_op jit(solution)/shard_map/ppermute | solution.py:17
  289.0 3.2 %collective-permute-start.30 = (f32[1,128,256]{2,1,0:T(8,128)S(1)}, f32[1,128,256]{2,1,0:T(8,128)S(1)}, u32[]{:S(2)}, u32[]{:S(2)}) collective-permute-start(f32[1,128,256]{2,1,0:T(8,128)S(1)} %slice.323), channel_id=1, source_target_pairs={{2,0},{4,2},{6,4},{8,6},{10,8},{12,10},{14,12},{16,14},{18,16},{20... | collective-permute-start | bytes 393224 | tf_op jit(solution)/shard_map/ppermute | solution.py:17
  296.4 2.1 collective-permute-start.31
  301.1 6.4 %collective-permute-done.31 = f32[1,128,256]{2,1,0:T(8,128)S(1)} collective-permute-done((f32[1,128,256]{2,1,0:T(8,128)S(1)}, f32[1,128,256]{2,1,0:T(8,128)S(1)}, u32[]{:S(2)}, u32[]{:S(2)}) %collective-permute-start.31) | collective-permute-done | bytes 131104 | tf_op jit(solution)/shard_map/ppermute | solution.py:17
  307.5 1.9 fusion.20
  (162 shorter events, 68.9 us)
Async XLA Ops:
  7.2 114.1 %all-gather.3.cloned.1.call-start = ((), (), s32[]{:S(2)}) async-start(), calls=%async_computation | async-start | bytes 33816576 | tf_op jit(solution)/shard_map/all_gather | solution.py:46
  12.5 138.0 %collective-permute-start = (f32[1,128,256]{2,1,0:T(8,128)S(1)}, f32[1,128,256]{2,1,0:T(8,128)S(1)}, u32[]{:S(2)}, u32[]{:S(2)}) collective-permute-start(f32[1,128,256]{2,1,0:T(8,128)S(1)} %slice.200), channel_id=1, source_target_pairs={{0,2},{2,4},{4,6},{6,8},{8,10},{10,12},{12,14},{14,16},{16,18},{18... | collective-permute-start | bytes 393224 | tf_op jit(solution)/shard_map/ppermute | solution.py:17
  15.9 134.6 %collective-permute-start.1 = (f32[8,1,256]{2,1,0:T(1,128)S(1)}, f32[8,1,256]{2,1,0:T(1,128)S(1)}, u32[]{:S(2)}, u32[]{:S(2)}) collective-permute-start(f32[8,1,256]{2,1,0:T(1,128)S(1)} %slice.201), channel_id=1, source_target_pairs={{0,1},{2,3},{4,5},{6,7},{8,9},{10,11},{12,13},{14,15},{16,17},{18,... | collective-permute-start | bytes 24584 | tf_op jit(solution)/shard_map/ppermute | solution.py:17
  154.0 8.5 %collective-permute-start.2 = (f32[1,128,256]{2,1,0:T(8,128)S(1)}, f32[1,128,256]{2,1,0:T(8,128)S(1)}, u32[]{:S(2)}, u32[]{:S(2)}) collective-permute-start(f32[1,128,256]{2,1,0:T(8,128)S(1)} %slice.267), channel_id=1, source_target_pairs={{2,0},{4,2},{6,4},{8,6},{10,8},{12,10},{14,12},{16,14},{18,16},{20... | collective-permute-start | bytes 393224 | tf_op jit(solution)/shard_map/ppermute | solution.py:17
  159.4 3.1 collective-permute-start.4
  163.0 11.7 %collective-permute-start.3 = (f32[1,128,256]{2,1,0:T(8,128)S(1)}, f32[1,128,256]{2,1,0:T(8,128)S(1)}, u32[]{:S(2)}, u32[]{:S(2)}) collective-permute-start(f32[1,128,256]{2,1,0:T(8,128)S(1)} %slice.268), channel_id=1, source_target_pairs={{0,2},{2,4},{4,6},{6,8},{8,10},{10,12},{12,14},{14,16},{16,18},{18... | collective-permute-start | bytes 393224 | tf_op jit(solution)/shard_map/ppermute | solution.py:17
  175.0 6.9 %collective-permute-start.6 = (f32[1,128,256]{2,1,0:T(8,128)S(1)}, f32[1,128,256]{2,1,0:T(8,128)S(1)}, u32[]{:S(2)}, u32[]{:S(2)}) collective-permute-start(f32[1,128,256]{2,1,0:T(8,128)S(1)} %slice.275), channel_id=1, source_target_pairs={{2,0},{4,2},{6,4},{8,6},{10,8},{12,10},{14,12},{16,14},{18,16},{20... | collective-permute-start | bytes 393224 | tf_op jit(solution)/shard_map/ppermute | solution.py:17
  178.8 3.1 collective-permute-start.8
  182.4 11.7 %collective-permute-start.7 = (f32[1,128,256]{2,1,0:T(8,128)S(1)}, f32[1,128,256]{2,1,0:T(8,128)S(1)}, u32[]{:S(2)}, u32[]{:S(2)}) collective-permute-start(f32[1,128,256]{2,1,0:T(8,128)S(1)} %slice.276), channel_id=1, source_target_pairs={{0,2},{2,4},{4,6},{6,8},{8,10},{10,12},{12,14},{14,16},{16,18},{18... | collective-permute-start | bytes 393224 | tf_op jit(solution)/shard_map/ppermute | solution.py:17
  184.5 2.8 collective-permute-start.9
  194.5 6.9 %collective-permute-start.10 = (f32[1,128,256]{2,1,0:T(8,128)S(1)}, f32[1,128,256]{2,1,0:T(8,128)S(1)}, u32[]{:S(2)}, u32[]{:S(2)}) collective-permute-start(f32[1,128,256]{2,1,0:T(8,128)S(1)} %slice.283), channel_id=1, source_target_pairs={{2,0},{4,2},{6,4},{8,6},{10,8},{12,10},{14,12},{16,14},{18,16},{20... | collective-permute-start | bytes 393224 | tf_op jit(solution)/shard_map/ppermute | solution.py:17
  197.7 3.1 collective-permute-start.12
  201.9 11.1 %collective-permute-start.11 = (f32[1,128,256]{2,1,0:T(8,128)S(1)}, f32[1,128,256]{2,1,0:T(8,128)S(1)}, u32[]{:S(2)}, u32[]{:S(2)}) collective-permute-start(f32[1,128,256]{2,1,0:T(8,128)S(1)} %slice.284), channel_id=1, source_target_pairs={{0,2},{2,4},{4,6},{6,8},{8,10},{10,12},{12,14},{14,16},{16,18},{18... | collective-permute-start | bytes 393224 | tf_op jit(solution)/shard_map/ppermute | solution.py:17
  204.0 2.6 collective-permute-start.13
  213.3 6.9 %collective-permute-start.14 = (f32[1,128,256]{2,1,0:T(8,128)S(1)}, f32[1,128,256]{2,1,0:T(8,128)S(1)}, u32[]{:S(2)}, u32[]{:S(2)}) collective-permute-start(f32[1,128,256]{2,1,0:T(8,128)S(1)} %slice.291), channel_id=1, source_target_pairs={{2,0},{4,2},{6,4},{8,6},{10,8},{12,10},{14,12},{16,14},{18,16},{20... | collective-permute-start | bytes 393224 | tf_op jit(solution)/shard_map/ppermute | solution.py:17
  216.5 3.1 collective-permute-start.16
  220.7 11.1 %collective-permute-start.15 = (f32[1,128,256]{2,1,0:T(8,128)S(1)}, f32[1,128,256]{2,1,0:T(8,128)S(1)}, u32[]{:S(2)}, u32[]{:S(2)}) collective-permute-start(f32[1,128,256]{2,1,0:T(8,128)S(1)} %slice.292), channel_id=1, source_target_pairs={{0,2},{2,4},{4,6},{6,8},{8,10},{10,12},{12,14},{14,16},{16,18},{18... | collective-permute-start | bytes 393224 | tf_op jit(solution)/shard_map/ppermute | solution.py:17
  222.8 2.6 collective-permute-start.17
  232.2 6.9 %collective-permute-start.18 = (f32[1,128,256]{2,1,0:T(8,128)S(1)}, f32[1,128,256]{2,1,0:T(8,128)S(1)}, u32[]{:S(2)}, u32[]{:S(2)}) collective-permute-start(f32[1,128,256]{2,1,0:T(8,128)S(1)} %slice.299), channel_id=1, source_target_pairs={{2,0},{4,2},{6,4},{8,6},{10,8},{12,10},{14,12},{16,14},{18,16},{20... | collective-permute-start | bytes 393224 | tf_op jit(solution)/shard_map/ppermute | solution.py:17
  235.4 3.1 collective-permute-start.20
  239.7 11.1 %collective-permute-start.19 = (f32[1,128,256]{2,1,0:T(8,128)S(1)}, f32[1,128,256]{2,1,0:T(8,128)S(1)}, u32[]{:S(2)}, u32[]{:S(2)}) collective-permute-start(f32[1,128,256]{2,1,0:T(8,128)S(1)} %slice.300), channel_id=1, source_target_pairs={{0,2},{2,4},{4,6},{6,8},{8,10},{10,12},{12,14},{14,16},{16,18},{18... | collective-permute-start | bytes 393224 | tf_op jit(solution)/shard_map/ppermute | solution.py:17
  241.8 2.6 collective-permute-start.21
  251.1 6.9 %collective-permute-start.22 = (f32[1,128,256]{2,1,0:T(8,128)S(1)}, f32[1,128,256]{2,1,0:T(8,128)S(1)}, u32[]{:S(2)}, u32[]{:S(2)}) collective-permute-start(f32[1,128,256]{2,1,0:T(8,128)S(1)} %slice.307), channel_id=1, source_target_pairs={{2,0},{4,2},{6,4},{8,6},{10,8},{12,10},{14,12},{16,14},{18,16},{20... | collective-permute-start | bytes 393224 | tf_op jit(solution)/shard_map/ppermute | solution.py:17
  254.3 3.1 collective-permute-start.24
  258.6 11.1 %collective-permute-start.23 = (f32[1,128,256]{2,1,0:T(8,128)S(1)}, f32[1,128,256]{2,1,0:T(8,128)S(1)}, u32[]{:S(2)}, u32[]{:S(2)}) collective-permute-start(f32[1,128,256]{2,1,0:T(8,128)S(1)} %slice.308), channel_id=1, source_target_pairs={{0,2},{2,4},{4,6},{6,8},{8,10},{10,12},{12,14},{14,16},{16,18},{18... | collective-permute-start | bytes 393224 | tf_op jit(solution)/shard_map/ppermute | solution.py:17
  260.7 2.6 collective-permute-start.25
  270.1 6.9 %collective-permute-start.26 = (f32[1,128,256]{2,1,0:T(8,128)S(1)}, f32[1,128,256]{2,1,0:T(8,128)S(1)}, u32[]{:S(2)}, u32[]{:S(2)}) collective-permute-start(f32[1,128,256]{2,1,0:T(8,128)S(1)} %slice.315), channel_id=1, source_target_pairs={{2,0},{4,2},{6,4},{8,6},{10,8},{12,10},{14,12},{16,14},{18,16},{20... | collective-permute-start | bytes 393224 | tf_op jit(solution)/shard_map/ppermute | solution.py:17
  273.3 3.1 collective-permute-start.28
  277.5 11.1 %collective-permute-start.27 = (f32[1,128,256]{2,1,0:T(8,128)S(1)}, f32[1,128,256]{2,1,0:T(8,128)S(1)}, u32[]{:S(2)}, u32[]{:S(2)}) collective-permute-start(f32[1,128,256]{2,1,0:T(8,128)S(1)} %slice.316), channel_id=1, source_target_pairs={{0,2},{2,4},{4,6},{6,8},{8,10},{10,12},{12,14},{14,16},{16,18},{18... | collective-permute-start | bytes 393224 | tf_op jit(solution)/shard_map/ppermute | solution.py:17
  289.0 6.9 %collective-permute-start.30 = (f32[1,128,256]{2,1,0:T(8,128)S(1)}, f32[1,128,256]{2,1,0:T(8,128)S(1)}, u32[]{:S(2)}, u32[]{:S(2)}) collective-permute-start(f32[1,128,256]{2,1,0:T(8,128)S(1)} %slice.323), channel_id=1, source_target_pairs={{2,0},{4,2},{6,4},{8,6},{10,8},{12,10},{14,12},{16,14},{18,16},{20... | collective-permute-start | bytes 393224 | tf_op jit(solution)/shard_map/ppermute | solution.py:17
  292.2 3.1 collective-permute-start.32
  296.4 11.1 %collective-permute-start.31 = (f32[1,128,256]{2,1,0:T(8,128)S(1)}, f32[1,128,256]{2,1,0:T(8,128)S(1)}, u32[]{:S(2)}, u32[]{:S(2)}) collective-permute-start(f32[1,128,256]{2,1,0:T(8,128)S(1)} %slice.324), channel_id=1, source_target_pairs={{0,2},{2,4},{4,6},{6,8},{8,10},{10,12},{12,14},{14,16},{16,18},{18... | collective-permute-start | bytes 393224 | tf_op jit(solution)/shard_map/ppermute | solution.py:17
  (6 other events, 292.1 us)
Sparse Core Ops, SparseCore 0:
  12.6 108.5 all-gather.2
